TPU v7x, 256 devices: a whole 4x4x8 slice. The times are simulated.
256 devices in a mesh: seq: 16 (over z, x_lo), wr: 4 (over y), wc: 4 (over x_hi, core).
Axes of the slice: x: 4 (x_hi: 2, x_lo: 2; x = x_hi * 2 + x_lo), y: 4, z: 8, core: 2. Of those that a mesh axis runs over, the one named last changes fastest.
Arguments:
- tokens: bfloat16 [8192, 2048], P('seq', ('wr', 'wc')), may hold values from -6 to 6
- ln_gain: float32 [2, 2048], replicated, may hold values from 0.5 to 1.5
- w_branch: bfloat16 [2, 2048, 4096], P(None, None, ('wr', 'wc')), may hold values from -0.125 to 0.125
- w_outgate: bfloat16 [2, 2048, 4096], P(None, None, ('wr', 'wc')), may hold values from -0.125 to 0.125
- w_gates: bfloat16 [2, 2048, 8], replicated, may hold values from -0.125 to 0.125
- forget_bias: float32 [2, 4], replicated, may hold values from 3.2 to 11
- conv_weight: float32 [2, 4, 4096], P(None, None, ('wr', 'wc')), may hold values from -3 to 3
- conv_bias: float32 [2, 4096], P(None, ('wr', 'wc')), may hold values from -3 to 3
- w_query: float32 [2, 4, 4, 4, 256], P(None, 'wr'), may hold values from -3 to 3
- w_key: float32 [2, 4, 4, 4, 256], P(None, 'wr'), may hold values from -3 to 3
- w_value: float32 [2, 4, 4, 4, 256], P(None, 'wr', None, 'wc'), may hold values from -4 to 4
- skip_gain: float32 [2, 4096], P(None, ('wr', 'wc')), may hold values from 0.5 to 1.5
- norm_gain: float32 [2, 4096], P(None, ('wr', 'wc')), may hold values from 0.5 to 1.5
- w_down: bfloat16 [2, 4096, 2048], P(None, ('wr', 'wc')), may hold values from -0.125 to 0.125
- lengths: int32 [3], replicated, may hold values from 1 to 4096, 8192 in all
- request_prompt: int32 [32], P('seq'), may hold values from 0 to 2
Outputs:
- mixed: bfloat16 [8192, 2048], P('seq', ('wr', 'wc'))
- request_state: bfloat16 [2, 32, 4, 1024, 1024], P(None, 'seq', 'wr', None, 'wc')
- request_conv: bfloat16 [2, 32, 3, 4096], P(None, 'seq', None, ('wr', 'wc'))
Inputs may be any that keep to these rules, and one draw needn't show every extreme that they name: `lengths`: the 3 prompts lie end to end in order and fill all 8192 positions; the longest has exactly 4096 positions.
All inputs are finite; a program needn't handle non-finite values.
Results may differ from a plain program's by a relative error of at most 0.035.
Values may be sent and summed in bfloat16 or wider, within the bound.
A program may use at most 128 MiB of HBM per device.

v0:
```python
import jax
import jax.numpy as jnp
from jax import lax
from jax.sharding import PartitionSpec as P

HEADS = 4
CONV = 4
LAYERS = 2
PROMPTS = 3
EPSILON = 1e-05
GATE_CAP = 15.0
ROW_DIMS = (((0,), (0,)), ((), ()))
FEATURE_DIMS = (((1,), (1,)), ((), ()))


def shifted(value, axis, steps):
    count = lax.axis_size(axis)
    first, last = (max(0, -steps), min(count, count - steps))
    return lax.ppermute(value, axis, [(source, source + steps) for source in range(first, last)])


def span_weights(gathered, lengths, rows, count):
    spans = jnp.arange(count, dtype=jnp.int32)
    seg_end = segment_of(spans * rows + (rows - 1), lengths)
    totals = gathered[:, 0]
    later = jnp.arange(count + 1, dtype=jnp.int32)
    between = (spans[None, None, :] > spans[None, :, None]) & (
        spans[None, None, :] < later[:, None, None]
    )
    logs = jnp.sum(jnp.where(between, totals[None, None, :], 0.0), axis=2)
    seg_in = segment_of(later * rows - 1, lengths)
    keep = (spans[None, :] < later[:, None]) & (seg_end[None, :] == seg_in[:, None])
    state_rows = jnp.where(keep, jnp.exp(logs), 0.0)
    end_rows = []
    for prompt, end_pos in enumerate((lengths[0] - 1, lengths[0] + lengths[1] - 1)):
        holder = end_pos // rows
        pick = (spans == holder).astype(jnp.float32)
        end_cum = jnp.sum(pick * gathered[:, 1 + prompt])
        row = jnp.sum(pick[:, None] * logs[:count], axis=0) + end_cum
        kept = (spans < holder) & (seg_end == prompt)
        kept = kept & (segment_of(holder * rows - 1, lengths) == prompt)
        end_rows.append(jnp.where(kept, jnp.exp(row), 0.0))
    return (state_rows[:count], jnp.stack(end_rows + [state_rows[count]]))


def mix_spans(weights, spans):
    return jnp.sum(weights[:, :, None, None] * spans[None], axis=1)


def norm_rows(source, gain_row):
    widened = source.astype(jnp.float32)
    row_mean = jnp.mean(widened, axis=1, keepdims=True)
    row_var = jnp.mean(widened * widened, axis=1, keepdims=True) - row_mean * row_mean
    return ((widened - row_mean) * lax.rsqrt(row_var + EPSILON) * gain_row).astype(jnp.bfloat16)


def segment_of(positions, lengths):
    bound_one = lengths[0]
    bound_two = lengths[0] + lengths[1]
    return (positions >= bound_one).astype(jnp.int32) + (positions >= bound_two).astype(jnp.int32)


def conv_rows(extended, ext_segment, segment, weight, bias_row):
    row_count = segment.shape[0]
    widened = extended.astype(jnp.float32)
    summed = jnp.zeros((row_count, widened.shape[1]), jnp.float32) + bias_row
    for back_step in range(weight.shape[0]):
        low_row = weight.shape[0] - 1 - back_step
        keep_row = (ext_segment[low_row : low_row + row_count] == segment).astype(jnp.float32)
        summed = (
            summed + weight[back_step] * widened[low_row : low_row + row_count] * keep_row[:, None]
        )
    return jax.nn.silu(summed).astype(jnp.bfloat16)


def block_mix(source, weight):
    row_count = source.shape[0]
    grouped = source.astype(jnp.float32).reshape(row_count, 4, -1)
    mixed = jnp.einsum("tig,ijg->tjg", grouped, weight, precision=lax.Precision.HIGHEST)
    return mixed.reshape(row_count, -1)


def block_terms(queries, key_rows, values, log_forget, in_gate, segment, prev_seg):
    row_count = queries.shape[0]
    cum_log = jnp.cumsum(log_forget)
    row_order = jnp.arange(row_count)
    allowed = (row_order[:, None] >= row_order[None, :]) & (segment[:, None] == segment[None, :])
    exponent = jnp.where(allowed, cum_log[:, None] - cum_log[None, :] + in_gate[None, :], -jnp.inf)
    scores = lax.dot_general(
        queries, key_rows, FEATURE_DIMS, preferred_element_type=jnp.float32
    ) * jnp.exp(exponent)
    in_block = jnp.dot(scores.astype(jnp.bfloat16), values, preferred_element_type=jnp.float32)
    carried = jnp.where(segment == prev_seg, jnp.exp(cum_log), 0.0)
    last_seg = segment[row_count - 1]
    weights = jnp.where(
        segment == last_seg, jnp.exp(cum_log[row_count - 1] - cum_log + in_gate), 0.0
    )
    weighted = (key_rows.astype(jnp.float32) * weights[:, None]).astype(jnp.bfloat16)
    increment = lax.dot_general(weighted, values, ROW_DIMS, preferred_element_type=jnp.float32)
    return (in_block, carried, increment)


def end_part(key_rows, values, cum_log, in_gate, segment, local_end, prompt, holder):
    row_order = jnp.arange(segment.shape[0])
    chosen = holder & (segment == prompt) & (row_order <= local_end)
    weights = jnp.where(chosen, jnp.exp(cum_log[local_end] - cum_log + in_gate), 0.0)
    weighted = (key_rows.astype(jnp.float32) * weights[:, None]).astype(jnp.bfloat16)
    return lax.dot_general(weighted, values, ROW_DIMS, preferred_element_type=jnp.float32)


def body(
    tokens,
    ln_gain,
    w_branch,
    w_outgate,
    w_gates,
    forget_bias,
    conv_weight,
    conv_bias,
    w_query,
    w_key,
    w_value,
    skip_gain,
    norm_gain,
    w_down,
    lengths,
    request_prompt,
):
    tok_rows = tokens.shape[0]
    seq_count = lax.axis_size("seq")
    seq_index = lax.axis_index("seq")
    head_idx = lax.axis_index("wr")
    row_offset = seq_index * tok_rows
    total_rows = tok_rows * seq_count
    row_ids = jnp.arange(tok_rows, dtype=jnp.int32)
    positions = row_offset + row_ids
    segment = segment_of(positions, lengths)
    seg_before = jnp.where(row_offset > 0, segment_of(row_offset - 1, lengths), -1)
    rim_positions = row_offset - (CONV - 1) + jnp.arange(CONV - 1, dtype=jnp.int32)
    rim_segment = jnp.where(rim_positions >= 0, segment_of(rim_positions, lengths), -1)
    ext_segment = jnp.concatenate([rim_segment, segment])
    prompt_starts = [jnp.zeros((), jnp.int32), lengths[0], lengths[0] + lengths[1]]
    prompt_ends = [
        lengths[0] - 1,
        lengths[0] + lengths[1] - 1,
        jnp.zeros((), jnp.int32) + (total_rows - 1),
    ]
    head_mask = (jnp.arange(HEADS, dtype=jnp.int32) == head_idx).astype(jnp.float32)
    current = tokens
    sent_states = []
    sent_edges = []
    for layer_idx in range(LAYERS):
        gathered = lax.all_gather(current, ("wr", "wc"), axis=1, tiled=True)
        normed = norm_rows(gathered, ln_gain[layer_idx])
        branch = jnp.dot(normed, w_branch[layer_idx], preferred_element_type=jnp.float32).astype(
            jnp.bfloat16
        )
        outgate = jnp.dot(normed, w_outgate[layer_idx], preferred_element_type=jnp.float32)
        gate_pre = jnp.dot(normed, w_gates[layer_idx], preferred_element_type=jnp.float32)
        input_pre = jnp.sum(gate_pre[:, :HEADS] * head_mask, axis=1)
        forget_pre = jnp.sum((gate_pre[:, HEADS:] + forget_bias[layer_idx]) * head_mask, axis=1)
        in_gate = GATE_CAP * jnp.tanh(input_pre / GATE_CAP)
        log_forget = jax.nn.log_sigmoid(forget_pre)
        edge_in = shifted(branch[tok_rows - (CONV - 1) :], "seq", 1)
        extended = jnp.concatenate([edge_in, branch], axis=0)
        conv_act = conv_rows(
            extended, ext_segment, segment, conv_weight[layer_idx], conv_bias[layer_idx]
        )
        head_branch, head_act = (
            lax.all_gather(branch, "wc", axis=1, tiled=True),
            lax.all_gather(conv_act, "wc", axis=1, tiled=True),
        )
        head_width = head_act.shape[1]
        queries = block_mix(head_act, w_query[layer_idx, 0]).astype(jnp.bfloat16)
        key_rows = (block_mix(head_act, w_key[layer_idx, 0]) * head_width ** (-0.5)).astype(
            jnp.bfloat16
        )
        values = block_mix(head_branch, w_value[layer_idx, 0]).astype(jnp.bfloat16)
        cum_log = jnp.cumsum(log_forget)
        holders = [
            (end_pos >= row_offset) & (end_pos < row_offset + tok_rows) for end_pos in prompt_ends
        ]
        local_ends = [jnp.clip(end_pos - row_offset, 0, tok_rows - 1) for end_pos in prompt_ends]
        span_logs = lax.all_gather(
            jnp.stack([cum_log[tok_rows - 1], cum_log[local_ends[0]], cum_log[local_ends[1]]]),
            "seq",
        )
        state_rows, end_rows = span_weights(span_logs, lengths, tok_rows, seq_count)
        in_block, carried, increment = block_terms(
            queries, key_rows, values, log_forget, in_gate, segment, seg_before
        )
        parts = [increment] + [
            end_part(
                key_rows,
                values,
                cum_log,
                in_gate,
                segment,
                local_ends[prompt],
                prompt,
                holders[prompt],
            )
            for prompt in range(PROMPTS - 1)
        ]
        slab = head_width // seq_count
        sent = jnp.stack(
            [part.astype(jnp.bfloat16).reshape(seq_count, slab, -1) for part in parts], axis=1
        )
        got = lax.all_to_all(sent, "seq", 0, 0, tiled=True).astype(jnp.float32)
        spans = got[:, 0]
        states = mix_spans(state_rows, spans).astype(jnp.bfloat16)
        state_here = lax.all_to_all(states, "seq", 0, 0, tiled=True).reshape(head_width, -1)
        own_ends = jnp.sum(got[:, 1:], axis=0)
        ends = mix_spans(end_rows, spans) + jnp.concatenate(
            [own_ends, jnp.zeros_like(own_ends[:1])], axis=0
        )
        sent_states.append(lax.all_gather(ends.astype(jnp.bfloat16), "seq", axis=1, tiled=True))
        hidden_parts = in_block + carried[:, None] * jnp.dot(
            queries, state_here, preferred_element_type=jnp.float32
        )
        sums_one, sums_two = lax.psum(
            (jnp.sum(hidden_parts, axis=1), jnp.sum(hidden_parts * hidden_parts, axis=1)), "wc"
        )
        row_mean = sums_one / head_width
        row_var = sums_two / head_width - row_mean * row_mean
        normal_rows = (hidden_parts - row_mean[:, None]) * lax.rsqrt(row_var + EPSILON)[:, None]
        gated = (
            (
                normal_rows * norm_gain[layer_idx]
                + skip_gain[layer_idx] * conv_act.astype(jnp.float32)
            )
            * jax.nn.silu(outgate)
        ).astype(jnp.bfloat16)
        term_rows = jnp.dot(gated, w_down[layer_idx], preferred_element_type=jnp.float32)
        terms = lax.all_to_all(
            term_rows.astype(jnp.bfloat16), ("wr", "wc"), 1, 0, tiled=True
        ).reshape(-1, tok_rows, current.shape[1])
        summed = jnp.sum(terms.astype(jnp.float32), axis=0)
        current = (current.astype(jnp.float32) + summed).astype(jnp.bfloat16)
        for prompt in range(PROMPTS):
            window = lax.dynamic_slice_in_dim(extended, local_ends[prompt] + 1, CONV - 1, 0)
            edge_pos = prompt_ends[prompt] - (CONV - 2) + jnp.arange(CONV - 1, dtype=jnp.int32)
            sent_edges.append(
                jnp.where(
                    ((edge_pos >= prompt_starts[prompt]) & holders[prompt])[:, None],
                    window,
                    jnp.zeros_like(window),
                )
            )
    state_stack = jnp.stack(sent_states)
    edge_stack = lax.psum(jnp.stack(sent_edges), "seq")
    edge_stack = edge_stack.reshape(LAYERS, PROMPTS, edge_stack.shape[1], edge_stack.shape[2])
    chooser = (request_prompt[:, None] == jnp.arange(PROMPTS, dtype=jnp.int32)[None, :]).astype(
        jnp.bfloat16
    )
    request_state = jnp.einsum(
        "rp,lphd->lrhd", chooser, state_stack, preferred_element_type=jnp.float32
    ).astype(jnp.bfloat16)[:, :, None]
    request_conv = jnp.einsum(
        "rp,lpkc->lrkc", chooser, edge_stack, preferred_element_type=jnp.float32
    ).astype(jnp.bfloat16)
    return (current, request_state, request_conv)


def solution(mesh):
    return jax.shard_map(
        body,
        mesh=mesh,
        in_specs=(
            P("seq", ("wr", "wc")),
            P(),
            P(None, None, ("wr", "wc")),
            P(None, None, ("wr", "wc")),
            P(),
            P(),
            P(None, None, ("wr", "wc")),
            P(None, ("wr", "wc")),
            P(None, "wr", None, None, None),
            P(None, "wr", None, None, None),
            P(None, "wr", None, "wc", None),
            P(None, ("wr", "wc")),
            P(None, ("wr", "wc")),
            P(None, ("wr", "wc"), None),
            P(),
            P("seq"),
        ),
        out_specs=(
            P("seq", ("wr", "wc")),
            P(None, "seq", "wr", None, "wc"),
            P(None, "seq", None, ("wr", "wc")),
        ),
        check_vma=False,
    )
```

profile of v0, /device:TPU:16, one launch (start us, length us, event | category | flops | bytes accessed | tf_op | source)
XLA Modules:
  0.0 664.2 jit_solution(5510766327636577990)
XLA Ops:
  14.5 49.2 %all-gather.11.cloned.1.call-done = bf16[512,2048]{1,0:T(8,128)(2,1)} async-done(((bf16[512,128]{1,0:T(8,128)(2,1)}), bf16[512,2048]{1,0:T(8,128)(2,1)}) %all-gather.11.cloned.1.call-update) | async-done | bytes 2097168 | tf_op jit(solution)/shard_map/all_gather | solution.py:153
  83.3 3.7 exponential_select_fusion.7
  86.9 5.6 all-gather.15.cloned.1.call-done
  96.0 21.3 %all-gather.13.cloned.1.call-done = bf16[512,1024]{1,0:T(8,128)(2,1)} async-done(((bf16[512,256]{1,0:T(8,128)(2,1)}), bf16[512,1024]{1,0:T(8,128)(2,1)}) %all-gather.13.cloned.1.call-update) | async-done | bytes 1048592 | tf_op jit(solution)/shard_map/all_gather | solution.py:171
  120.5 3.3 fusion.74
  136.0 7.3 %all-to-all-start = ((bf16[16,3,64,256]{3,2,1,0:T(8,128)(2,1)}), bf16[16,3,64,256]{3,2,1,0:T(8,128)(2,1)}, u32[]{:S(2)}, u32[]{:S(2)}) async-start(bf16[16,3,64,256]{3,2,1,0:T(8,128)(2,1)} %pad_maximum_fusion.6), calls=%async_computation | async-start | bytes 3145728 | tf_op jit(solution)/shard_map/all_to_all | solution.py:209
  149.7 56.5 %all-reduce.2 = f32[48]{0:T(128)S(1)} all-reduce(f32[48]{0:T(128)S(1)} %maximum_dynamic-update-slice_fusion), channel_id=2, replica_groups=mesh['seq'=16,'wr'=4,'wc'=4] {'seq'}, use_global_device_ids=true, to_apply=%add.2 | all-reduce | flops 48 | bytes 384
  213.4 6.7 %all-to-all-start.1 = ((bf16[16,64,256]{2,1,0:T(8,128)(2,1)}), bf16[16,64,256]{2,1,0:T(8,128)(2,1)}, u32[]{:S(2)}, u32[]{:S(2)}) async-start(bf16[16,64,256]{2,1,0:T(8,128)(2,1)} %multiply_reduce_fusion.1), calls=%async_computation.1 | async-start | bytes 1048576 | tf_op jit(solution)/shard_map/all_to_all | solution.py:212
  221.4 3.2 fusion.21
  226.8 3.5 fusion.28
  230.4 3.3 all-to-all-done.1
  236.5 7.1 %all-reduce.5 = (f32[512]{0:T(512)S(1)}, f32[512]{0:T(512)S(1)}) all-reduce(f32[512]{0:T(512)S(1)} %get-tuple-element.28, f32[512]{0:T(512)S(1)} %get-tuple-element.27), channel_id=1, replica_groups=mesh['seq'=16,'wr'=4,'wc'=4] {'wc'}, use_global_device_ids=true, to_apply=%region_11.12 | all-reduce | flops 1024 | bytes 8192 | tf_op jit(solution)/shard_map/psum | solution.py:221
  243.6 6.0 fusion.17
  251.8 32.7 %all_to_all.46 = bf16[512,16,128]{2,0,1:T(8,128)(2,1)S(1)} all-to-all(bf16[512,16,128]{2,0,1:T(8,128)(2,1)S(1)} %bitcast.288), channel_id=1, replica_groups=mesh['seq'=16,'wr'=4,'wc'=4] {'wr','wc'}, dimensions={1} | all-to-all | bytes 4194304 | tf_op jit(solution)/shard_map/all_to_all | solution.py:235
  286.4 46.1 %all-gather.17.cloned.1.call-done = bf16[512,2048]{1,0:T(8,128)(2,1)} async-done(((bf16[512,128]{1,0:T(8,128)(2,1)}), bf16[512,2048]{1,0:T(8,128)(2,1)}) %all-gather.17.cloned.1.call-update) | async-done | bytes 2097168 | tf_op jit(solution)/shard_map/all_gather | solution.py:153
  353.7 8.2 %all-gather.21.cloned.1.call-done = bf16[512,1024]{1,0:T(8,128)(2,1)} async-done(((bf16[512,256]{1,0:T(8,128)(2,1)}), bf16[512,1024]{1,0:T(8,128)(2,1)}) %all-gather.21.cloned.1.call-update) | async-done | bytes 1048592 | tf_op jit(solution)/shard_map/all_gather | solution.py:170
  364.5 3.4 multiply_reduce_fusion.4
  369.0 17.5 %all-gather.19.cloned.1.call-done = bf16[512,1024]{1,0:T(8,128)(2,1)} async-done(((bf16[512,256]{1,0:T(8,128)(2,1)}), bf16[512,1024]{1,0:T(8,128)(2,1)}) %all-gather.19.cloned.1.call-update) | async-done | bytes 1048592 | tf_op jit(solution)/shard_map/all_gather | solution.py:171
  389.1 3.8 copy.199
  392.9 4.5 fusion.71
  421.6 7.3 %all-to-all-start.3 = ((bf16[16,3,64,256]{3,2,1,0:T(8,128)(2,1)}), bf16[16,3,64,256]{3,2,1,0:T(8,128)(2,1)}, u32[]{:S(2)}, u32[]{:S(2)}) async-start(bf16[16,3,64,256]{3,2,1,0:T(8,128)(2,1)} %pad_maximum_fusion.7), calls=%async_computation.3 | async-start | bytes 3145728 | tf_op jit(solution)/shard_map/all_to_all | solution.py:209
  433.7 58.0 %all-reduce.3 = f32[48]{0:T(128)S(1)} all-reduce(f32[48]{0:T(128)S(1)} %maximum_dynamic-update-slice_fusion.1), channel_id=3, replica_groups=mesh['seq'=16,'wr'=4,'wc'=4] {'seq'}, use_global_device_ids=true, to_apply=%add.3 | all-reduce | flops 48 | bytes 384
  509.2 6.8 %all-to-all-start.4 = ((bf16[16,64,256]{2,1,0:T(8,128)(2,1)}), bf16[16,64,256]{2,1,0:T(8,128)(2,1)}, u32[]{:S(2)}, u32[]{:S(2)}) async-start(bf16[16,64,256]{2,1,0:T(8,128)(2,1)} %multiply_reduce_fusion), calls=%async_computation.4 | async-start | bytes 1048576 | tf_op jit(solution)/shard_map/all_to_all | solution.py:212
  516.0 3.2 fusion.22
  521.5 3.6 fusion.27
  527.5 4.4 all-to-all-done.4
  534.0 7.2 %all-reduce.4 = (f32[512]{0:T(512)S(1)}, f32[512]{0:T(512)S(1)}) all-reduce(f32[512]{0:T(512)S(1)} %get-tuple-element.26, f32[512]{0:T(512)S(1)} %get-tuple-element.25), channel_id=1, replica_groups=mesh['seq'=16,'wr'=4,'wc'=4] {'wc'}, use_global_device_ids=true, to_apply=%region_24.25 | all-reduce | flops 1024 | bytes 8192 | tf_op jit(solution)/shard_map/psum | solution.py:221
  541.3 5.2 fusion.18
  546.5 3.5 copy.268
  550.0 7.6 %all-to-all-start.5 = ((bf16[512,16,128]{2,0,1:T(8,128)(2,1)}), bf16[512,16,128]{2,0,1:T(8,128)(2,1)S(1)}, u32[]{:S(2)}, u32[]{:S(2)}) async-start(bf16[512,16,128]{2,0,1:T(8,128)(2,1)} %bitcast.287), calls=%async_computation.5 | async-start | bytes 4194304 | tf_op jit(solution)/shard_map/all_to_all | solution.py:235
  559.4 84.2 %psum.39 = bf16[2,3,3,256]{3,1,2,0:T(4,128)(2,1)S(1)} all-reduce(bf16[2,3,3,256]{3,1,2,0:T(4,128)(2,1)S(1)} %copy.221), channel_id=1, replica_groups=mesh['seq'=16,'wr'=4,'wc'=4] {'seq'}, use_global_device_ids=true, to_apply=%region_38.39 | all-reduce | flops 4608 | bytes 18432 | tf_op jit(solution)/shard_map/psum | solution.py:251
  644.5 4.1 copy.271
  (322 shorter events, 155.5 us)
Async XLA Ops:
  7.2 56.5 %all-gather.11.cloned.1.call-start = ((), (), s32[]{:S(2)}) async-start(), calls=%async_computation.6 | async-start | bytes 2228224 | tf_op jit(solution)/shard_map/all_gather | solution.py:153
  7.9 84.7 %all-gather.15.cloned.1.call-start = ((), (), s32[]{:S(2)}) async-start(), calls=%async_computation.8 | async-start | bytes 1310720 | tf_op jit(solution)/shard_map/all_gather | solution.py:170
  12.5 63.7 %copy-start.36 = (s32[512]{0:T(512)}, s32[512]{0:T(512)S(1)}, u32[]{:S(2)}) copy-start(s32[512]{0:T(512)S(1)} %convert_add_fusion) | copy-start | bytes 6148
  67.8 12.2 %copy-start.5 = (bf16[512,2048]{1,0:T(8,128)(2,1)}, bf16[512,2048]{1,0:T(8,128)(2,1)S(1)}, u32[]{:S(2)}) copy-start(bf16[512,2048]{1,0:T(8,128)(2,1)S(1)} %fusion.2) | copy-start | bytes 6291460
  69.2 48.1 %all-gather.13.cloned.1.call-start = ((), (), s32[]{:S(2)}) async-start(), calls=%async_computation.7 | async-start | bytes 1310720 | tf_op jit(solution)/shard_map/all_gather | solution.py:171
  72.5 5.3 collective-permute-start
  80.0 14.5 %copy-start.54 = (f32[4]{0:T(128)}, f32[4]{0:T(128)S(1)}, u32[]{:S(2)}) copy-start(f32[4]{0:T(128)S(1)} %compare_convert_fusion.6) | copy-start | bytes 52
  136.0 71.3 %all-to-all-start = ((bf16[16,3,64,256]{3,2,1,0:T(8,128)(2,1)}), bf16[16,3,64,256]{3,2,1,0:T(8,128)(2,1)}, u32[]{:S(2)}, u32[]{:S(2)}) async-start(bf16[16,3,64,256]{3,2,1,0:T(8,128)(2,1)} %pad_maximum_fusion.6), calls=%async_computation | async-start | bytes 3145728 | tf_op jit(solution)/shard_map/all_to_all | solution.py:209
  146.9 60.4 %copy-start.50 = (s32[17]{0:T(128)}, s32[17]{0:T(128)S(1)}, u32[]{:S(2)}) copy-start(s32[17]{0:T(128)S(1)} %fusion.170) | copy-start | bytes 208
  147.6 59.7 %copy-start.52 = (s32[16]{0:T(128)}, s32[16]{0:T(128)S(1)}, u32[]{:S(2)}) copy-start(s32[16]{0:T(128)S(1)} %fusion.169) | copy-start | bytes 196
  147.6 59.5 %copy-start.31 = (pred[17,16]{0,1:T(8,128)(4,1)}, pred[17,16]{0,1:T(8,128)(4,1)S(1)}, u32[]{:S(2)}) copy-start(pred[17,16]{0,1:T(8,128)(4,1)S(1)} %iota_compare_fusion.2) | copy-start | bytes 820
  147.6 59.5 %copy-start.32 = (pred[16,16]{1,0:T(8,128)(4,1)}, pred[16,16]{1,0:T(8,128)(4,1)S(1)}, u32[]{:S(2)}) copy-start(pred[16,16]{1,0:T(8,128)(4,1)S(1)} %iota_compare_fusion.1) | copy-start | bytes 772
  209.2 11.7 %copy-start.61 = (f32[2,256]{1,0:T(2,128)S(1)}, f32[2,256]{1,0:T(2,128)}, u32[]{:S(2)}) copy-start(f32[2,256]{1,0:T(2,128)} %param.28) | copy-start | bytes 6148
  213.4 20.2 %all-to-all-start.1 = ((bf16[16,64,256]{2,1,0:T(8,128)(2,1)}), bf16[16,64,256]{2,1,0:T(8,128)(2,1)}, u32[]{:S(2)}, u32[]{:S(2)}) async-start(bf16[16,64,256]{2,1,0:T(8,128)(2,1)} %multiply_reduce_fusion.1), calls=%async_computation.1 | async-start | bytes 1048576 | tf_op jit(solution)/shard_map/all_to_all | solution.py:212
  220.2 112.3 %all-gather.17.cloned.1.call-start = ((), (), s32[]{:S(2)}) async-start(), calls=%async_computation.9 | async-start | bytes 2228224 | tf_op jit(solution)/shard_map/all_gather | solution.py:153
  230.4 13.3 %copy-start.20 = (bf16[512,256]{1,0:T(8,128)(2,1)S(1)}, bf16[512,256]{1,0:T(8,128)(2,1)}, u32[]{:S(2)}) copy-start(bf16[512,256]{1,0:T(8,128)(2,1)} %multiply_convert_fusion.5) | copy-start | bytes 786436
  286.1 75.8 %all-gather.21.cloned.1.call-start = ((), (), s32[]{:S(2)}) async-start(), calls=%async_computation.11 | async-start | bytes 1310720 | tf_op jit(solution)/shard_map/all_gather | solution.py:170
  338.5 47.9 %all-gather.19.cloned.1.call-start = ((), (), s32[]{:S(2)}) async-start(), calls=%async_computation.10 | async-start | bytes 1310720 | tf_op jit(solution)/shard_map/all_gather | solution.py:171
  339.2 3.8 collective-permute-start.1
  350.6 38.5 %copy-start.34 = (f32[512]{0:T(512)}, f32[512]{0:T(512)S(1)}, u32[]{:S(2)}) copy-start(f32[512]{0:T(512)S(1)} %get-tuple-element.54) | copy-start | bytes 6148
  421.6 81.6 %all-to-all-start.3 = ((bf16[16,3,64,256]{3,2,1,0:T(8,128)(2,1)}), bf16[16,3,64,256]{3,2,1,0:T(8,128)(2,1)}, u32[]{:S(2)}, u32[]{:S(2)}) async-start(bf16[16,3,64,256]{3,2,1,0:T(8,128)(2,1)} %pad_maximum_fusion.7), calls=%async_computation.3 | async-start | bytes 3145728 | tf_op jit(solution)/shard_map/all_to_all | solution.py:209
  428.9 215.6 %all-gather.23.cloned.1.call-start = ((), (), s32[]{:S(2)}) async-start(), calls=%async_computation.12 | async-start | bytes 1671168 | tf_op jit(solution)/shard_map/all_gather | solution.py:217
  431.7 69.2 %copy-start.51 = (s32[17]{0:T(128)S(1)}, s32[17]{0:T(128)}, u32[]{:S(2)}) copy-start(s32[17]{0:T(128)} %copy-done.50) | copy-start | bytes 208
  431.7 69.2 %copy-start.53 = (s32[16]{0:T(128)S(1)}, s32[16]{0:T(128)}, u32[]{:S(2)}) copy-start(s32[16]{0:T(128)} %copy-done.52) | copy-start | bytes 196
  509.2 22.7 %all-to-all-start.4 = ((bf16[16,64,256]{2,1,0:T(8,128)(2,1)}), bf16[16,64,256]{2,1,0:T(8,128)(2,1)}, u32[]{:S(2)}, u32[]{:S(2)}) async-start(bf16[16,64,256]{2,1,0:T(8,128)(2,1)} %multiply_reduce_fusion), calls=%async_computation.4 | async-start | bytes 1048576 | tf_op jit(solution)/shard_map/all_to_all | solution.py:212
  516.0 134.2 %all-gather.25.cloned.1.call-start = ((), (), s32[]{:S(2)}) async-start(), calls=%async_computation.13 | async-start | bytes 1671168 | tf_op jit(solution)/shard_map/all_gather | solution.py:217
  526.8 14.5 %copy-start.4 = (bf16[512,2048]{1,0:T(8,128)(2,1)S(1)}, bf16[512,2048]{1,0:T(8,128)(2,1)}, u32[]{:S(2)}) copy-start(bf16[512,2048]{1,0:T(8,128)(2,1)} %copy-done.3) | copy-start | bytes 6291460
  526.8 14.5 %copy-start.19 = (bf16[512,256]{1,0:T(8,128)(2,1)S(1)}, bf16[512,256]{1,0:T(8,128)(2,1)}, u32[]{:S(2)}) copy-start(bf16[512,256]{1,0:T(8,128)(2,1)} %multiply_convert_fusion.3) | copy-start | bytes 786436
  526.8 14.5 %copy-start.66 = (f32[1,256]{1,0:T(1,128)S(1)}, f32[1,256]{1,0:T(1,128)}, u32[]{:S(2)}) copy-start(f32[1,256]{1,0:T(1,128)} %get-tuple-element.102) | copy-start | bytes 3076
  526.8 14.5 %copy-start.67 = (f32[1,256]{1,0:T(1,128)S(1)}, f32[1,256]{1,0:T(1,128)}, u32[]{:S(2)}) copy-start(f32[1,256]{1,0:T(1,128)} %get-tuple-element.100) | copy-start | bytes 3076
  550.0 93.7 %copy-start.70 = (s32[2]{0:T(128)S(1)}, s32[2]{0:T(128)}, u32[]{:S(2)}) copy-start(s32[2]{0:T(128)} %param.31) | copy-start | bytes 28
  550.0 98.6 %all-to-all-start.5 = ((bf16[512,16,128]{2,0,1:T(8,128)(2,1)}), bf16[512,16,128]{2,0,1:T(8,128)(2,1)S(1)}, u32[]{:S(2)}, u32[]{:S(2)}) async-start(bf16[512,16,128]{2,0,1:T(8,128)(2,1)} %bitcast.287), calls=%async_computation.5 | async-start | bytes 4194304 | tf_op jit(solution)/shard_map/all_to_all | solution.py:235
  (55 other events, 284.2 us)
Sparse Core Ops, SparseCore 0:
  10.6 53.0 all-gather.10
  69.3 23.1 all-gather.14
  94.4 22.8 all-gather.12
  286.2 46.2 all-gather.16
  338.6 23.1 all-gather.20
  363.5 22.8 all-gather.18
  499.2 73.1 all-gather.22
  574.1 70.0 all-gather.24
where the time goes:
time: 669 us; the launch traced here: 664 us
  blocking collectives  246 us (37%)
  waiting for transfers between devices  158 us (24%)
  local copies, waits for them, and re-layouts  72 us (11%)
  other arithmetic  69.9 us (10%)
  matrix products  56.6 us (8%)
  starting transfers between devices  41.7 us (6%)
  between operations  20.6 us (3%)
    unnamed x2, blocking collectives  114 us
    all_gather x2, waiting for transfers between devices, body(): gathered = lax.all_gather(current, ('wr', 'wc'), axis=1, tiled=True)  95.3 us
    psum x1, blocking collectives, body(): edge_stack = lax.psum(jnp.stack(sent_edges), 'seq')  84.2 us
    all_gather x2, waiting for transfers between devices, body(): lax.all_gather(conv_act, 'wc', axis=1, tiled=True)  38.8 us
    all_to_all x1, blocking collectives, body(): lax.all_to_all(term_rows.astype(jnp.bfloat16), ('wr', 'wc'), 1, 0, tiled=...  32.7 us
    unnamed x154, local copies, waits for them, and re-layouts  15 us
    all_to_all x2, starting transfers between devices, body(): got = lax.all_to_all(sent, 'seq', 0, 0, tiled=True).astype(jnp.float32)  14.6 us
    psum x2, blocking collectives, body(): lax.psum((jnp.sum(hidden_parts, axis=1), jnp.sum(hidden_parts * hidden_pa...  14.3 us
  transfers between devices with their start and end apart: 15, of which 9 were waited for; matrix products, arithmetic and copies ran while one was open for 16% of the time, Pallas kernels for 0%

commit v1 on v0

--- a/solution.py
+++ b/solution.py
@@ -168,7 +168,12 @@
         )
         head_branch, head_act = (
             lax.all_gather(branch, "wc", axis=1, tiled=True),
-            lax.all_gather(conv_act, "wc", axis=1, tiled=True),
+            jnp.concatenate(
+                lax.all_to_all(
+                    jnp.stack([conv_act for _ in range(lax.axis_size("wc"))]), "wc", 0, 0
+                ),
+                axis=1,
+            ),
         )
         head_width = head_act.shape[1]
         queries = block_mix(head_act, w_query[layer_idx, 0]).astype(jnp.bfloat16)

time: 669 us -> 650 us (0.972); the launches traced: 664 us -> 638 us
  waiting for transfers between devices: 158 us -> 125 us
  starting transfers between devices: 41.7 us -> 50.2 us
    all_gather x2 -> x0, waiting for transfers between devices: 38.8 us -> none  [body(): lax.all_gather(conv_act, 'wc', axis=1, tiled=True)]
    all_to_all x0 -> x2, waiting for transfers between devices: none -> 29.1 us  [body(): lax.all_to_all(jnp.stack([conv_act for _ in range(lax.axis_size('wc'))]),...]
    all_gather x2, waiting for transfers between devices: 13.8 us -> 0.01 us  [body(): lax.all_gather(branch, 'wc', axis=1, tiled=True)]
    all_gather x2, waiting for transfers between devices: 95.3 us -> 86 us  [body(): gathered = lax.all_gather(current, ('wr', 'wc'), axis=1, tiled=True)]
    reshape x6 -> x2, local copies, waits for them, and re-layouts: 14.2 us -> 5.33 us  [block_mix(): grouped = source.astype(jnp.float32).reshape(row_count, 4, -1)]
    all_to_all x0 -> x2, starting transfers between devices: none -> 7.79 us  [body(): lax.all_to_all(jnp.stack([conv_act for _ in range(lax.axis_size('wc'))]),...]
    unnamed x154 -> x148, local copies, waits for them, and re-layouts: 15 us -> 15.5 us
  transfers between devices with their start and end apart: 15 -> 15, of which waited for: 9 -> 8; matrix products, arithmetic and copies ran while one was open for 16% -> 21% of each run, Pallas kernels for 0% -> 0%
where the time goes in v1:
time: 650 us; the launch traced here: 638 us
  blocking collectives  243 us (37%)
  waiting for transfers between devices  125 us (19%)
  local copies, waits for them, and re-layouts  75.4 us (12%)
  other arithmetic  71.6 us (11%)
  matrix products  52 us (8%)
  starting transfers between devices  50.2 us (8%)
  between operations  20.9 us (3%)
    unnamed x2, blocking collectives  112 us
    all_gather x2, waiting for transfers between devices, body(): gathered = lax.all_gather(current, ('wr', 'wc'), axis=1, tiled=True)  86 us
    psum x1, blocking collectives, body(): edge_stack = lax.psum(jnp.stack(sent_edges), 'seq')  83.6 us
    all_to_all x1, blocking collectives, body(): lax.all_to_all(term_rows.astype(jnp.bfloat16), ('wr', 'wc'), 1, 0, tiled=...  32.2 us
    all_to_all x2, waiting for transfers between devices, body(): lax.all_to_all(jnp.stack([conv_act for _ in range(lax.axis_size('wc'))]),...  29.1 us
    all_to_all x2, starting transfers between devices, body(): got = lax.all_to_all(sent, 'seq', 0, 0, tiled=True).astype(jnp.float32)  17.4 us
    dot_general x4, matrix products, block_mix(): jnp.einsum('tig,ijg->tjg', grouped, weight, precision=lax.Precision.HIGHEST)  15.5 us
    unnamed x148, local copies, waits for them, and re-layouts  15.5 us
  transfers between devices with their start and end apart: 15, of which 8 were waited for; matrix products, arithmetic and copies ran while one was open for 21% of the time, Pallas kernels for 0%

profile of v1, /device:TPU:16, one launch (start us, length us, event | category | flops | bytes accessed | tf_op | source)
XLA Modules:
  0.0 638.1 jit_solution(16768068108584327377)
XLA Ops:
  22.4 41.3 %all-gather.9.cloned.1.call-done = bf16[512,2048]{1,0:T(8,128)(2,1)} async-done(((bf16[512,128]{1,0:T(8,128)(2,1)}), bf16[512,2048]{1,0:T(8,128)(2,1)}) %all-gather.9.cloned.1.call-update) | async-done | bytes 2097168 | tf_op jit(solution)/shard_map/all_gather | solution.py:153
  76.1 3.5 all-to-all-start
  82.2 3.8 exponential_select_fusion.7
  86.0 15.1 %all-to-all-done = bf16[4,512,256]{1,2,0:T(8,128)(2,1)S(1)} async-done(((bf16[4,512,256]{1,2,0:T(8,128)(2,1)}), bf16[4,512,256]{1,2,0:T(8,128)(2,1)S(1)}, u32[]{:S(2)}, u32[]{:S(2)}) %all-to-all-start) | async-done | bytes 1048608 | tf_op jit(solution)/shard_map/all_to_all | solution.py:172
  101.1 3.6 fusion.60
  125.4 8.5 %all-to-all-start.1 = ((bf16[16,3,64,256]{3,2,1,0:T(8,128)(2,1)}), bf16[16,3,64,256]{3,2,1,0:T(8,128)(2,1)}, u32[]{:S(2)}, u32[]{:S(2)}) async-start(bf16[16,3,64,256]{3,2,1,0:T(8,128)(2,1)} %pad_maximum_fusion.6), calls=%async_computation.1 | async-start | bytes 3145728 | tf_op jit(solution)/shard_map/all_to_all | solution.py:214
  140.4 55.9 %all-reduce.2 = f32[48]{0:T(128)S(1)} all-reduce(f32[48]{0:T(128)S(1)} %maximum_dynamic-update-slice_fusion), channel_id=2, replica_groups=mesh['seq'=16,'wr'=4,'wc'=4] {'seq'}, use_global_device_ids=true, to_apply=%add.2 | all-reduce | flops 48 | bytes 384
  200.5 3.2 multiply_reduce_fusion.1
  203.6 6.9 %all-to-all-start.2 = ((bf16[16,64,256]{2,1,0:T(8,128)(2,1)}), bf16[16,64,256]{2,1,0:T(8,128)(2,1)}, u32[]{:S(2)}, u32[]{:S(2)}) async-start(bf16[16,64,256]{2,1,0:T(8,128)(2,1)} %multiply_reduce_fusion.1), calls=%async_computation.2 | async-start | bytes 1048576 | tf_op jit(solution)/shard_map/all_to_all | solution.py:217
  211.7 3.6 fusion.21
  217.4 3.6 fusion.28
  226.8 7.1 %all-reduce.5 = (f32[512]{0:T(512)S(1)}, f32[512]{0:T(512)S(1)}) all-reduce(f32[512]{0:T(512)S(1)} %get-tuple-element.28, f32[512]{0:T(512)S(1)} %get-tuple-element.27), channel_id=1, replica_groups=mesh['seq'=16,'wr'=4,'wc'=4] {'wc'}, use_global_device_ids=true, to_apply=%region_11.12 | all-reduce | flops 1024 | bytes 8192 | tf_op jit(solution)/shard_map/psum | solution.py:226
  233.9 6.1 fusion.17
  242.2 32.2 %all_to_all.56 = bf16[512,16,128]{2,0,1:T(8,128)(2,1)S(1)} all-to-all(bf16[512,16,128]{2,0,1:T(8,128)(2,1)S(1)} %bitcast.284), channel_id=1, replica_groups=mesh['seq'=16,'wr'=4,'wc'=4] {'wr','wc'}, dimensions={1} | all-to-all | bytes 4194304 | tf_op jit(solution)/shard_map/all_to_all | solution.py:240
  278.0 44.7 %all-gather.13.cloned.1.call-done = bf16[512,2048]{1,0:T(8,128)(2,1)} async-done(((bf16[512,128]{1,0:T(8,128)(2,1)}), bf16[512,2048]{1,0:T(8,128)(2,1)}) %all-gather.13.cloned.1.call-update) | async-done | bytes 2097168 | tf_op jit(solution)/shard_map/all_gather | solution.py:153
  340.3 4.3 all-to-all-start.4
  348.8 14.0 %all-to-all-done.4 = bf16[4,512,256]{1,2,0:T(8,128)(2,1)} async-done(((bf16[4,512,256]{1,2,0:T(8,128)(2,1)}), bf16[4,512,256]{1,2,0:T(8,128)(2,1)}, u32[]{:S(2)}, u32[]{:S(2)}) %all-to-all-start.4) | async-done | bytes 1048608 | tf_op jit(solution)/shard_map/all_to_all | solution.py:172
  362.8 4.9 fusion.57
  370.7 3.2 fusion.14
  386.3 3.3 multiply_reduce_fusion.4
  396.9 8.8 %all-to-all-start.5 = ((bf16[16,3,64,256]{3,2,1,0:T(8,128)(2,1)}), bf16[16,3,64,256]{3,2,1,0:T(8,128)(2,1)}, u32[]{:S(2)}, u32[]{:S(2)}) async-start(bf16[16,3,64,256]{3,2,1,0:T(8,128)(2,1)} %pad_maximum_fusion.7), calls=%async_computation.5 | async-start | bytes 3145728 | tf_op jit(solution)/shard_map/all_to_all | solution.py:214
  411.7 56.2 %all-reduce.3 = f32[48]{0:T(128)S(1)} all-reduce(f32[48]{0:T(128)S(1)} %maximum_dynamic-update-slice_fusion.1), channel_id=3, replica_groups=mesh['seq'=16,'wr'=4,'wc'=4] {'seq'}, use_global_device_ids=true, to_apply=%add.3 | all-reduce | flops 48 | bytes 384
  484.8 6.7 %all-to-all-start.6 = ((bf16[16,64,256]{2,1,0:T(8,128)(2,1)}), bf16[16,64,256]{2,1,0:T(8,128)(2,1)}, u32[]{:S(2)}, u32[]{:S(2)}) async-start(bf16[16,64,256]{2,1,0:T(8,128)(2,1)} %multiply_reduce_fusion), calls=%async_computation.6 | async-start | bytes 1048576 | tf_op jit(solution)/shard_map/all_to_all | solution.py:217
  491.6 3.5 fusion.22
  497.3 3.6 fusion.27
  503.4 4.0 all-to-all-done.6
  509.6 7.6 %all-reduce.4 = (f32[512]{0:T(512)S(1)}, f32[512]{0:T(512)S(1)}) all-reduce(f32[512]{0:T(512)S(1)} %get-tuple-element.26, f32[512]{0:T(512)S(1)} %get-tuple-element.25), channel_id=1, replica_groups=mesh['seq'=16,'wr'=4,'wc'=4] {'wc'}, use_global_device_ids=true, to_apply=%region_24.25 | all-reduce | flops 1024 | bytes 8192 | tf_op jit(solution)/shard_map/psum | solution.py:226
  517.3 5.2 fusion.18
  522.5 3.5 copy.280
  526.0 6.0 all-to-all-start.7
  533.9 83.6 %psum.39 = bf16[2,3,3,256]{3,1,2,0:T(4,128)(2,1)S(1)} all-reduce(bf16[2,3,3,256]{3,1,2,0:T(4,128)(2,1)S(1)} %copy.225), channel_id=1, replica_groups=mesh['seq'=16,'wr'=4,'wc'=4] {'seq'}, use_global_device_ids=true, to_apply=%region_38.39 | all-reduce | flops 4608 | bytes 18432 | tf_op jit(solution)/shard_map/psum | solution.py:256
  618.3 4.1 copy.283
  (315 shorter events, 155.4 us)
Async XLA Ops:
  7.2 56.5 %all-gather.9.cloned.1.call-start = ((), (), s32[]{:S(2)}) async-start(), calls=%async_computation.8 | async-start | bytes 2228224 | tf_op jit(solution)/shard_map/all_gather | solution.py:153
  7.9 108.9 %all-gather.11.cloned.1.call-start = ((), (), s32[]{:S(2)}) async-start(), calls=%async_computation.9 | async-start | bytes 1310720 | tf_op jit(solution)/shard_map/all_gather | solution.py:170
  15.8 57.2 %copy-start.52 = (f32[4]{0:T(128)}, f32[4]{0:T(128)S(1)}, u32[]{:S(2)}) copy-start(f32[4]{0:T(128)S(1)} %compare_convert_fusion.6) | copy-start | bytes 52
  20.1 54.4 %copy-start.24 = (f32[512]{0:T(512)}, f32[512]{0:T(512)S(1)}, u32[]{:S(2)}) copy-start(f32[512]{0:T(512)S(1)} %get-tuple-element.95) | copy-start | bytes 6148
  20.1 54.4 %copy-start.26 = (f32[512]{0:T(512)}, f32[512]{0:T(512)S(1)}, u32[]{:S(2)}) copy-start(f32[512]{0:T(512)S(1)} %get-tuple-element.96) | copy-start | bytes 6148
  20.1 54.4 %copy-start.28 = (f32[512]{0:T(512)}, f32[512]{0:T(512)S(1)}, u32[]{:S(2)}) copy-start(f32[512]{0:T(512)S(1)} %get-tuple-element.97) | copy-start | bytes 6148
  70.6 3.8 collective-permute-start
  76.1 25.0 %all-to-all-start = ((bf16[4,512,256]{1,2,0:T(8,128)(2,1)}), bf16[4,512,256]{1,2,0:T(8,128)(2,1)S(1)}, u32[]{:S(2)}, u32[]{:S(2)}) async-start(bf16[4,512,256]{1,2,0:T(8,128)(2,1)} %stack.66), calls=%async_computation | async-start | bytes 2097152 | tf_op jit(solution)/shard_map/all_to_all | solution.py:172
  81.5 25.1 %copy-start.34 = (f32[512]{0:T(512)}, f32[512]{0:T(512)S(1)}, u32[]{:S(2)}) copy-start(f32[512]{0:T(512)S(1)} %get-tuple-element.59) | copy-start | bytes 6148
  125.4 72.2 %all-to-all-start.1 = ((bf16[16,3,64,256]{3,2,1,0:T(8,128)(2,1)}), bf16[16,3,64,256]{3,2,1,0:T(8,128)(2,1)}, u32[]{:S(2)}, u32[]{:S(2)}) async-start(bf16[16,3,64,256]{3,2,1,0:T(8,128)(2,1)} %pad_maximum_fusion.6), calls=%async_computation.1 | async-start | bytes 3145728 | tf_op jit(solution)/shard_map/all_to_all | solution.py:214
  137.5 59.9 %copy-start.48 = (s32[17]{0:T(128)}, s32[17]{0:T(128)S(1)}, u32[]{:S(2)}) copy-start(s32[17]{0:T(128)S(1)} %fusion.174) | copy-start | bytes 208
  138.2 59.2 %copy-start.50 = (s32[16]{0:T(128)}, s32[16]{0:T(128)S(1)}, u32[]{:S(2)}) copy-start(s32[16]{0:T(128)S(1)} %fusion.173) | copy-start | bytes 196
  138.3 59.0 %copy-start.30 = (pred[17,16]{0,1:T(8,128)(4,1)}, pred[17,16]{0,1:T(8,128)(4,1)S(1)}, u32[]{:S(2)}) copy-start(pred[17,16]{0,1:T(8,128)(4,1)S(1)} %iota_compare_fusion.2) | copy-start | bytes 820
  138.3 59.0 %copy-start.31 = (pred[16,16]{1,0:T(8,128)(4,1)}, pred[16,16]{1,0:T(8,128)(4,1)S(1)}, u32[]{:S(2)}) copy-start(pred[16,16]{1,0:T(8,128)(4,1)S(1)} %iota_compare_fusion.1) | copy-start | bytes 772
  203.6 20.4 %all-to-all-start.2 = ((bf16[16,64,256]{2,1,0:T(8,128)(2,1)}), bf16[16,64,256]{2,1,0:T(8,128)(2,1)}, u32[]{:S(2)}, u32[]{:S(2)}) async-start(bf16[16,64,256]{2,1,0:T(8,128)(2,1)} %multiply_reduce_fusion.1), calls=%async_computation.2 | async-start | bytes 1048576 | tf_op jit(solution)/shard_map/all_to_all | solution.py:217
  210.5 112.2 %all-gather.13.cloned.1.call-start = ((), (), s32[]{:S(2)}) async-start(), calls=%async_computation.10 | async-start | bytes 2228224 | tf_op jit(solution)/shard_map/all_gather | solution.py:153
  276.0 107.6 %all-gather.15.cloned.1.call-start = ((), (), s32[]{:S(2)}) async-start(), calls=%async_computation.11 | async-start | bytes 1310720 | tf_op jit(solution)/shard_map/all_gather | solution.py:170
  330.5 3.8 collective-permute-start.1
  340.3 22.6 %all-to-all-start.4 = ((bf16[4,512,256]{1,2,0:T(8,128)(2,1)}), bf16[4,512,256]{1,2,0:T(8,128)(2,1)}, u32[]{:S(2)}, u32[]{:S(2)}) async-start(bf16[4,512,256]{1,2,0:T(8,128)(2,1)} %stack.69), calls=%async_computation.4 | async-start | bytes 2097152 | tf_op jit(solution)/shard_map/all_to_all | solution.py:172
  345.8 24.9 %copy-start.32 = (f32[512]{0:T(512)}, f32[512]{0:T(512)S(1)}, u32[]{:S(2)}) copy-start(f32[512]{0:T(512)S(1)} %get-tuple-element.54) | copy-start | bytes 6148
  396.9 81.8 %all-to-all-start.5 = ((bf16[16,3,64,256]{3,2,1,0:T(8,128)(2,1)}), bf16[16,3,64,256]{3,2,1,0:T(8,128)(2,1)}, u32[]{:S(2)}, u32[]{:S(2)}) async-start(bf16[16,3,64,256]{3,2,1,0:T(8,128)(2,1)} %pad_maximum_fusion.7), calls=%async_computation.5 | async-start | bytes 3145728 | tf_op jit(solution)/shard_map/all_to_all | solution.py:214
  405.8 212.6 %all-gather.17.cloned.1.call-start = ((), (), s32[]{:S(2)}) async-start(), calls=%async_computation.12 | async-start | bytes 1671168 | tf_op jit(solution)/shard_map/all_gather | solution.py:222
  409.7 66.8 %copy-start.49 = (s32[17]{0:T(128)S(1)}, s32[17]{0:T(128)}, u32[]{:S(2)}) copy-start(s32[17]{0:T(128)} %copy-done.48) | copy-start | bytes 208
  409.7 66.8 %copy-start.51 = (s32[16]{0:T(128)S(1)}, s32[16]{0:T(128)}, u32[]{:S(2)}) copy-start(s32[16]{0:T(128)} %copy-done.50) | copy-start | bytes 196
  484.8 22.6 %all-to-all-start.6 = ((bf16[16,64,256]{2,1,0:T(8,128)(2,1)}), bf16[16,64,256]{2,1,0:T(8,128)(2,1)}, u32[]{:S(2)}, u32[]{:S(2)}) async-start(bf16[16,64,256]{2,1,0:T(8,128)(2,1)} %multiply_reduce_fusion), calls=%async_computation.6 | async-start | bytes 1048576 | tf_op jit(solution)/shard_map/all_to_all | solution.py:217
  491.6 132.4 %all-gather.19.cloned.1.call-start = ((), (), s32[]{:S(2)}) async-start(), calls=%async_computation.13 | async-start | bytes 1671168 | tf_op jit(solution)/shard_map/all_gather | solution.py:222
  502.7 14.6 %copy-start.3 = (bf16[512,2048]{1,0:T(8,128)(2,1)S(1)}, bf16[512,2048]{1,0:T(8,128)(2,1)}, u32[]{:S(2)}) copy-start(bf16[512,2048]{1,0:T(8,128)(2,1)} %copy-done.2) | copy-start | bytes 6291460
  502.7 14.6 %copy-start.17 = (bf16[512,256]{1,0:T(8,128)(2,1)S(1)}, bf16[512,256]{1,0:T(8,128)(2,1)}, u32[]{:S(2)}) copy-start(bf16[512,256]{1,0:T(8,128)(2,1)} %multiply_convert_fusion.3) | copy-start | bytes 786436
  502.7 14.6 %copy-start.61 = (f32[1,256]{1,0:T(1,128)S(1)}, f32[1,256]{1,0:T(1,128)}, u32[]{:S(2)}) copy-start(f32[1,256]{1,0:T(1,128)} %get-tuple-element.102) | copy-start | bytes 3076
  502.7 14.6 %copy-start.62 = (f32[1,256]{1,0:T(1,128)S(1)}, f32[1,256]{1,0:T(1,128)}, u32[]{:S(2)}) copy-start(f32[1,256]{1,0:T(1,128)} %get-tuple-element.100) | copy-start | bytes 3076
  526.0 91.6 %copy-start.67 = (s32[2]{0:T(128)S(1)}, s32[2]{0:T(128)}, u32[]{:S(2)}) copy-start(s32[2]{0:T(128)} %param.31) | copy-start | bytes 28
  526.0 96.4 %all-to-all-start.7 = ((bf16[512,16,128]{2,0,1:T(8,128)(2,1)}), bf16[512,16,128]{2,0,1:T(8,128)(2,1)S(1)}, u32[]{:S(2)}, u32[]{:S(2)}) async-start(bf16[512,16,128]{2,0,1:T(8,128)(2,1)} %bitcast.283), calls=%async_computation.7 | async-start | bytes 4194304 | tf_op jit(solution)/shard_map/all_to_all | solution.py:240
  (52 other events, 291.0 us)
Sparse Core Ops, SparseCore 0:
  10.6 53.0 all-gather.8
  69.3 28.9 all-gather.10
  276.1 46.5 all-gather.12
  329.9 25.5 all-gather.14
  474.9 71.9 all-gather.16
  548.5 70.0 all-gather.18
